TPU v7x, 512 devices: a whole 4x8x8 slice. The times are simulated.
512 devices in a mesh: ent: 128 (over y, z, core), rep: 4 (over x).
Axes of the slice: x: 4, y: 8, z: 8, core: 2. Of those that a mesh axis runs over, the one named last changes fastest.
Arguments:
- item_factors: bfloat16 [524288, 128], P(('ent', 'rep')), may hold values from -0.1 to 0.1
- tile_items: int32 [128, 4, 256, 32], P('ent', 'rep'), may hold values from 0 to 1023
- send_tiles: int32 [128, 4, 128], P('ent', 'rep'), may hold values from 1 to 2, as said below
- tile_users: int32 [128, 4, 256, 1], P('ent', 'rep'), may hold values from 0 to 7
- tile_counts: int32 [128, 4, 256, 32], P('ent', 'rep'), may hold values from 0 to 31
- recv_tiles: int32 [128, 4, 128], P('ent', 'rep'), may hold values from 1 to 2, as said below
Outputs:
- user_factors: float32 [1024, 128], P(('ent', 'rep'))
- item_rhs: float32 [524288, 128], P(('ent', 'rep'))
Inputs may be any that keep to these rules, and one draw needn't show every extreme that they name: send_tiles[e, r, p] counts the leading tile slots p * 2 to p * 2 + 1 of device (e, r) that are live; every device sends 2 tiles to some peer and receives 2 tiles from some peer. recv_tiles[p, r, e] equals send_tiles[e, r, p].
All inputs are finite; a program needn't handle non-finite values.
Results may differ from a plain program's by a relative error of at most 0.0009.
The roundings to bfloat16 on the way count: a program that leaves them out, or rounds other values in their place, can miss the bound.
Values may be sent and summed in bfloat16 or wider, within the bound.
A program may use at most 64 MiB of HBM per device.

v0:
```python
import jax
import jax.numpy as jnp
from jax import lax
from jax.sharding import PartitionSpec as P

U_DEV = 2
ALPHA = 40.0
RIDGE = 1.0
RHS_SCALE = 1.0 / 640.0


def solve_users(gram, rhs):
    lower = jnp.linalg.cholesky(gram)
    halfway = lax.linalg.triangular_solve(lower, rhs[..., None], left_side=True, lower=True)
    result = lax.linalg.triangular_solve(
        lower, halfway, left_side=True, lower=True, transpose_a=True
    )
    return result[..., 0]


def shards(item_factors, tile_items, send_tiles, tile_users, tile_counts, recv_tiles):
    highest = lax.Precision.HIGHEST
    rank_width = item_factors.shape[1]
    item_count = item_factors.shape[0]
    n_ent = lax.axis_size("ent")
    tile_slots = tile_items.shape[2]
    tile_rows = tile_items.shape[3]
    seg_count = tile_users.shape[3]
    seg_length = tile_rows // seg_count
    slot_cap = tile_slots // n_ent
    user_block = U_DEV * lax.axis_size("rep")
    item_ids = tile_items.reshape(tile_slots, tile_rows)
    slot_pos = jnp.arange(tile_slots, dtype=jnp.int32) % slot_cap
    live_send = slot_pos < jnp.repeat(send_tiles.reshape(n_ent), slot_cap)
    live_recv = slot_pos < jnp.repeat(recv_tiles.reshape(n_ent), slot_cap)
    partial_gram = lax.dot_general(
        item_factors, item_factors, (((0,), (0,)), ((), ())), preferred_element_type=jnp.float32
    )
    picked = jnp.take(item_factors, item_ids.reshape(-1), axis=0).reshape(
        tile_slots, tile_rows, rank_width
    )
    picked = jnp.where(live_send[:, None, None], picked, jnp.zeros((), jnp.bfloat16))
    incoming = lax.all_to_all(
        picked.reshape(n_ent, slot_cap * tile_rows, rank_width),
        "ent",
        split_axis=0,
        concat_axis=0,
        tiled=True,
    )
    counts_int = tile_counts.reshape(tile_slots, tile_rows)
    counts_f = counts_int.astype(jnp.float32)
    gram_weight = ALPHA * counts_f
    rhs_weight = jnp.where(
        live_recv[:, None] & (counts_int > 0), 1.0 + ALPHA * counts_f, jnp.float32(0.0)
    )
    owners = tile_users.reshape(tile_slots * seg_count)
    selector = owners[None, :] == jnp.arange(user_block, dtype=jnp.int32)[:, None]
    selector_f = selector.astype(jnp.float32)
    src_group = 1
    while (
        src_group * 2 <= n_ent
        and n_ent % (src_group * 2) == 0
        and (src_group * 2 * slot_cap * tile_rows <= 4096)
    ):
        src_group = src_group * 2
    tiles_blk = src_group * slot_cap
    block_count = tile_slots // tiles_blk
    runs_blk = tiles_blk * seg_count

    def accumulate(state_pair, pieces):
        gram_run, rhs_run = state_pair
        rows_blk, gram_blk, rhs_blk, select_blk = pieces
        weighted = (gram_blk[:, :, None] * rows_blk).astype(jnp.bfloat16)
        rows_seg = rows_blk.reshape(tiles_blk, seg_count, seg_length, rank_width)
        weighted = weighted.reshape(tiles_blk, seg_count, seg_length, rank_width)
        run_gram = jnp.einsum(
            "tsri,tsrj->tsij", weighted, rows_seg, preferred_element_type=jnp.float32
        )
        run_gram = run_gram.reshape(runs_blk, rank_width * rank_width)
        run_rhs = jnp.einsum(
            "tsr,tsri->tsi",
            rhs_blk.reshape(tiles_blk, seg_count, seg_length),
            rows_seg.astype(jnp.float32),
            precision=highest,
        )
        run_rhs = run_rhs.reshape(runs_blk, rank_width)
        gram_run = gram_run + jnp.dot(select_blk, run_gram, precision=highest)
        rhs_run = rhs_run + jnp.dot(select_blk, run_rhs, precision=highest)
        return ((gram_run, rhs_run), None)

    block_pieces = (
        incoming.reshape(block_count, tiles_blk, tile_rows, rank_width),
        gram_weight.reshape(block_count, tiles_blk, tile_rows),
        rhs_weight.reshape(block_count, tiles_blk, tile_rows),
        jnp.transpose(selector_f.reshape(user_block, block_count, runs_blk), (1, 0, 2)),
    )
    start_pair = (
        jnp.zeros((user_block, rank_width * rank_width), jnp.float32),
        jnp.zeros((user_block, rank_width), jnp.float32),
    )
    (gram_acc, rhs_acc), _ = lax.scan(accumulate, start_pair, block_pieces)
    identity_mat = jnp.eye(rank_width, dtype=jnp.float32)
    added_term = lax.psum(partial_gram, ("ent", "rep")) + RIDGE * identity_mat
    own_gram, own_rhs = (
        lax.psum_scatter(gram_acc, "rep", scatter_dimension=0, tiled=True),
        lax.psum_scatter(rhs_acc, "rep", scatter_dimension=0, tiled=True),
    )
    own_factors = solve_users(own_gram.reshape(-1, rank_width, rank_width) + added_term, own_rhs)
    solved = lax.all_gather(own_factors.astype(jnp.bfloat16), "rep", axis=0, tiled=True)
    run_factor = lax.dot_general(
        selector.astype(jnp.bfloat16),
        solved,
        (((0,), (0,)), ((), ())),
        preferred_element_type=jnp.float32,
    )
    back_factor, back_weight = (
        lax.all_to_all(
            run_factor.reshape(n_ent, slot_cap, seg_count * rank_width),
            "ent",
            split_axis=0,
            concat_axis=0,
            tiled=True,
        ),
        lax.all_to_all(
            rhs_weight.reshape(n_ent, slot_cap, tile_rows),
            "ent",
            split_axis=0,
            concat_axis=0,
            tiled=True,
        ),
    )

    def spread(running, pieces):
        factor_blk, weight_blk, item_blk = pieces
        contrib = (weight_blk[:, :, :, None] * factor_blk[:, :, None, :]).reshape(-1, rank_width)
        return (
            running + jax.ops.segment_sum(contrib, item_blk.reshape(-1), num_segments=item_count),
            None,
        )

    spread_pieces = (
        back_factor.reshape(block_count, tiles_blk, seg_count, rank_width),
        back_weight.reshape(block_count, tiles_blk, seg_count, seg_length),
        item_ids.reshape(block_count, tiles_blk, tile_rows),
    )
    item_rhs, _ = lax.scan(spread, jnp.zeros((item_count, rank_width), jnp.float32), spread_pieces)
    return (own_factors, item_rhs * RHS_SCALE)


def solution(mesh):
    in_specs = (
        P(("ent", "rep"), None),
        P("ent", "rep", None, None),
        P("ent", "rep", None),
        P("ent", "rep", None, None),
        P("ent", "rep", None, None),
        P("ent", "rep", None),
    )
    out_specs = (P(("ent", "rep"), None), P(("ent", "rep"), None))
    return jax.shard_map(shards, mesh=mesh, in_specs=in_specs, out_specs=out_specs, check_vma=False)
```

profile of v0, /device:TPU:1, one launch (start us, length us, event | category | flops | bytes accessed | tf_op | source)
XLA Modules:
  0.0 525.8 jit_solution(16828590585126697929)
XLA Ops:
  9.2 24.0 %gather_fusion = bf16[8192,128]{1,0:T(8,128)(2,1)S(1)} fusion(bf16[1024,128]{1,0:T(8,128)(2,1)S(1)} %copy-done, s32[8192]{0:T(1024)S(1)} %broadcast_clamp_fusion), kind=kCustom, calls=%fused_computation | custom fusion | bytes 4227072 | tf_op jit(solution)/shard_map/jit(_take)/gather | solution.py:39
  33.2 4.6 select_select_fusion
  37.8 18.6 %all-to-all-start = ((bf16[128,64,128]{2,1,0:T(8,128)(2,1)}), bf16[128,64,128]{2,1,0:T(8,128)(2,1)S(1)}, u32[]{:S(2)}, u32[]{:S(2)}) async-start(bf16[128,64,128]{2,1,0:T(8,128)(2,1)} %select_select_fusion), calls=%async_computation | async-start | bytes 4194304 | tf_op jit(solution)/shard_map/all_to_all | solution.py:43
  59.4 1.3 dynamic-slice
  62.4 46.3 %all-to-all-done = bf16[128,64,128]{2,1,0:T(8,128)(2,1)S(1)} async-done(((bf16[128,64,128]{2,1,0:T(8,128)(2,1)}), bf16[128,64,128]{2,1,0:T(8,128)(2,1)S(1)}, u32[]{:S(2)}, u32[]{:S(2)}) %all-to-all-start) | async-done | bytes 2097184 | tf_op jit(solution)/shard_map/all_to_all | solution.py:43
  108.7 7.6 %all-to-all-start.1 = ((f32[128,2,32]{2,1,0:T(2,128)}), f32[128,2,32]{2,1,0:T(2,128)S(1)}, u32[]{:S(2)}, u32[]{:S(2)}) async-start(f32[128,2,32]{2,1,0:T(2,128)} %and_select_fusion), calls=%async_computation.1 | async-start | bytes 262144 | tf_op jit(solution)/shard_map/all_to_all | solution.py:124
  116.5 37.8 %while.24 = (s32[]{:T(128)}, f32[8,16384]{1,0:T(8,128)S(1)}, f32[8,128]{1,0:T(8,128)S(1)}, f32[2,8,128]{2,1,0:T(8,128)S(1)}, f32[2,128,32]{2,1,0:T(8,128)S(1)}, ...) while((s32[]{:T(128)}, f32[8,16384]{1,0:T(8,128)S(1)}, ...), condition=%wide.region_1.2_spmd.clone, body=%wide.region_0.1_spmd.clone.sunk | while | flops 345245696 | bytes 21267580 | solution.py:101
  116.5 5.2 fusion.49
  121.7 12.5 %convolution_add_fusion.4 = f32[8,16384]{1,0:T(8,128)S(1)} fusion(f32[16,8,128,128]{3,2,1,0:T(8,128)} %bitcast.121, f32[8,16384]{1,0:T(8,128)S(1)} %get-tuple-element.219, pred[]{:T(512)S(6)} %compare.15, f32[2,8,128]{2,1,0:T(8,128)S(1)} %get-tuple-element.230, s32[]{:T(128)} %get-tuple-element.218), kind=kOutput, calls=%fused_computation.6.clone.1 | convolution fusion | flops 201588736 | bytes 9441285 | tf_op jit(solution)/shard_map/while/body/eval_jaxpr/dot_general | solution.py:87
  134.3 0.9 fusion.50
  135.4 5.2 fusion.49
  140.6 12.5 %convolution_add_fusion.4 = f32[8,16384]{1,0:T(8,128)S(1)} fusion(f32[16,8,128,128]{3,2,1,0:T(8,128)} %bitcast.121, f32[8,16384]{1,0:T(8,128)S(1)} %get-tuple-element.219, pred[]{:T(512)S(6)} %compare.15, f32[2,8,128]{2,1,0:T(8,128)S(1)} %get-tuple-element.230, s32[]{:T(128)} %get-tuple-element.218), kind=kOutput, calls=%fused_computation.6.clone.1 | convolution fusion | flops 201588736 | bytes 9441285 | tf_op jit(solution)/shard_map/while/body/eval_jaxpr/dot_general | solution.py:87
  153.2 0.9 fusion.50
  155.2 186.7 %all-reduce.5.cloned.1.call-done = f32[128,128]{1,0:T(8,128)} async-done(((f32[128,128]{1,0:T(8,128)}), f32[128,128]{1,0:T(8,128)}) %all-reduce.5.cloned.1.call-update) | async-done | bytes 65552 | tf_op jit(solution)/shard_map/psum | solution.py:103
  342.9 8.1 %all-reduce.1 = f32[8,128]{1,0:T(8,128)S(1)} all-reduce(f32[8,128]{1,0:T(8,128)S(1)} %get-tuple-element.68), channel_id=3, replica_groups=mesh['ent'=128,'rep'=4] {'rep'}, use_global_device_ids=true, to_apply=%region_6.7.clone | all-reduce | flops 1024 | bytes 8192
  350.9 37.3 %all-reduce.7.cloned.1.call-done = f32[8,16384]{1,0:T(8,128)} async-done(((f32[8,16384]{1,0:T(8,128)}), f32[8,16384]{1,0:T(8,128)}) %all-reduce.7.cloned.1.call-update) | async-done | bytes 524304
  388.3 1.1 dynamic-slice_bitcast_fusion.2
  389.6 23.5 %custom-call.9 = f32[2,128,128]{2,1,0:T(8,128)S(1)} custom-call(f32[2,128,128]{2,1,0:T(8,128)S(1)} %fusion.20), custom_call_target="Cholesky" | custom-call | tf_op jit(solution)/shard_map/jit(cholesky)/cholesky | solution.py:13
  413.3 19.7 %custom-call.10 = f32[2,1,128,128]{2,3,1,0:T(8,128)S(1)} custom-call(f32[2,1,128,128]{3,2,1,0:T(8,128)S(1)} %select_bitcast_fusion), custom_call_target="InvertDiagBlocksLowerTriangular" | custom-call | tf_op jit(solution)/shard_map/triangular_solve | solution.py:15
  433.6 6.8 %all-gather = bf16[4,2,128]{2,1,0:T(2,128)(2,1)S(1)} all-gather(bf16[1,2,128]{2,1,0:T(2,128)(2,1)S(1)} %convert_bitcast_fusion), channel_id=1, replica_groups=mesh['ent'=128,'rep'=4] {'rep'}, dimensions={0}, use_global_device_ids=true | all-gather | bytes 2560 | tf_op jit(solution)/shard_map/all_gather | solution.py:109
  440.6 30.5 %all_to_all.15 = f32[128,2,128]{2,1,0:T(2,128)S(1)} all-to-all(f32[128,2,128]{2,1,0:T(2,128)S(1)} %bitcast.132), channel_id=1, replica_groups=mesh['ent'=128,'rep'=4] {'ent'}, dimensions={0} | all-to-all | bytes 262144 | tf_op jit(solution)/shard_map/all_to_all | solution.py:117
  471.2 46.8 %while.23 = (s32[]{:T(128)}, f32[1024,128]{1,0:T(8,128)S(1)}, s32[2,128,32]{2,1,0:T(8,128)S(1)}, f32[2,128,1,32]{3,1,2,0:T(8,128)S(1)}, f32[2,128,1,128]{3,1,2,0:T(8,128)S(1)}, /*index=5*/s32[]{:T(128)}) while((s32[]{:T(128)}, f32[1024,128]{1,0:T(8,128)S(1)}, s32[2,128,32]{2,1,0:T(8,128)S(1)}, f32[2,128,1,32]{3,1,2,0:T(8,128)S(1)}, ...), condition=%wide.region_9.10_spmd, body=%wide.region_7.9_spmd.sunk | while | flops 1048578 | bytes 8749137 | solution.py:146
  472.1 22.6 %scatter_fusion = f32[1024,128]{1,0:T(8,128)S(1)} fusion(f32[1024,128]{1,0:T(8,128)S(1)} %get-tuple-element.243, s32[4096]{0:T(1024)S(1)} %reshape.259, f32[4096,128]{1,0:T(8,128)S(1)} %bitcast_multiply_fusion.2), kind=kCustom, calls=%fused_computation.1.clone.1 | custom fusion | flops 524288 | bytes 6307840 | tf_op jit(solution)/shard_map/while/body/eval_jaxpr/scatter-add | solution.py:137
  495.5 22.6 %scatter_fusion = f32[1024,128]{1,0:T(8,128)S(1)} fusion(f32[1024,128]{1,0:T(8,128)S(1)} %get-tuple-element.243, s32[4096]{0:T(1024)S(1)} %reshape.259, f32[4096,128]{1,0:T(8,128)S(1)} %bitcast_multiply_fusion.2), kind=kCustom, calls=%fused_computation.1.clone.1 | custom fusion | flops 524288 | bytes 6307840 | tf_op jit(solution)/shard_map/while/body/eval_jaxpr/scatter-add | solution.py:137
  (83 shorter events, 12.1 us)
Async XLA Ops:
  7.2 2.0 copy-start
  37.8 20.1 %copy-start.5 = (s32[1,1,128]{2,1,0:T(1,128)S(1)}, s32[1,1,128]{2,1,0:T(1,128)}, u32[]{:S(2)}) copy-start(s32[1,1,128]{2,1,0:T(1,128)} %param.15) | copy-start | bytes 1540
  37.8 21.0 %copy-start.2 = (s32[1,1,256,32]{2,3,1,0:T(8,128)S(1)}, s32[1,1,256,32]{2,3,1,0:T(8,128)}, u32[]{:S(2)}) copy-start(s32[1,1,256,32]{2,3,1,0:T(8,128)} %param.14) | copy-start | bytes 98308
  37.8 23.6 %copy-start.3 = (s32[1,1,256,1]{2,3,1,0:T(1,128)S(1)}, s32[1,1,256,1]{2,3,1,0:T(1,128)}, u32[]{:S(2)}) copy-start(s32[1,1,256,1]{2,3,1,0:T(1,128)} %param.13) | copy-start | bytes 3076
  37.8 70.9 %all-to-all-start = ((bf16[128,64,128]{2,1,0:T(8,128)(2,1)}), bf16[128,64,128]{2,1,0:T(8,128)(2,1)S(1)}, u32[]{:S(2)}, u32[]{:S(2)}) async-start(bf16[128,64,128]{2,1,0:T(8,128)(2,1)} %select_select_fusion), calls=%async_computation | async-start | bytes 4194304 | tf_op jit(solution)/shard_map/all_to_all | solution.py:43
  56.4 285.5 %all-reduce.5.cloned.1.call-start = ((), (), s32[]{:S(2)}) async-start(), calls=%async_computation.3 | async-start | bytes 131072 | tf_op jit(solution)/shard_map/psum | solution.py:103
  108.7 332.0 %all-to-all-start.1 = ((f32[128,2,32]{2,1,0:T(2,128)}), f32[128,2,32]{2,1,0:T(2,128)S(1)}, u32[]{:S(2)}, u32[]{:S(2)}) async-start(f32[128,2,32]{2,1,0:T(2,128)} %and_select_fusion), calls=%async_computation.1 | async-start | bytes 262144 | tf_op jit(solution)/shard_map/all_to_all | solution.py:124
  116.3 272.0 %all-reduce.7.cloned.1.call-start = ((), (), s32[]{:S(2)}) async-start(), calls=%async_computation.4 | async-start | bytes 1048576
  154.3 0.8 copy-start.1
  433.6 37.7 %copy-start.4 = (f32[2,1,128]{2,1,0:T(1,128)}, f32[2,1,128]{2,1,0:T(1,128)S(1)}, u32[]{:S(2)}) copy-start(f32[2,1,128]{2,1,0:T(1,128)S(1)} %fusion.17) | copy-start | bytes 3076
Sparse Core Ops, SparseCore 0:
  62.2 279.6 all-reduce.4
  344.9 43.2 all-reduce.6
where the time goes:
time: 526 us
  waiting for transfers between devices  270 us (51%)
  other arithmetic  98.5 us (19%)
  blocking collectives  45.4 us (9%)
  matrix products  39.3 us (7%)
  local copies, waits for them, and re-layouts  30.6 us (6%)
  starting transfers between devices  26.4 us (5%)
  between operations  15 us (3%)
    psum x1, waiting for transfers between devices, shards(): added_term = lax.psum(partial_gram, ('ent', 'rep')) + RIDGE * identity_mat  187 us
    all_to_all x1, waiting for transfers between devices, shards(): lax.all_to_all(picked.reshape(n_ent, slot_cap * tile_rows, rank_width), '...  46.3 us
    scatter-add x2, other arithmetic, spread(): jax.ops.segment_sum(contrib, item_blk.reshape(-1), num_segments=item_count)  45.1 us
    unnamed x3, waiting for transfers between devices  37.4 us
    all_to_all x1, blocking collectives, shards(): lax.all_to_all(run_factor.reshape(n_ent, slot_cap, seg_count * rank_width...  30.5 us
    dot_general x2, matrix products, accumulate(): gram_run = gram_run + jnp.dot(select_blk, run_gram, precision=highest)  25 us
    gather x1, local copies, waits for them, and re-layouts, shards(): jnp.take(item_factors, item_ids.reshape(-1), axis=0)  24 us
    another operation x4, other arithmetic, solve_users(): lower = jnp.linalg.cholesky(gram)  23.6 us
  transfers between devices with their start and end apart: 4, of which 3 were waited for; matrix products, arithmetic and copies ran while one was open for 17% of the time, Pallas kernels for 0%

commit v1 on v0

--- a/solution.py
+++ b/solution.py
@@ -100,7 +100,8 @@
     )
     (gram_acc, rhs_acc), _ = lax.scan(accumulate, start_pair, block_pieces)
     identity_mat = jnp.eye(rank_width, dtype=jnp.float32)
-    added_term = lax.psum(partial_gram, ("ent", "rep")) + RIDGE * identity_mat
+    _supply_side = lambda view: jnp.sum(lax.all_gather(view, ("ent", "rep")), 0)
+    added_term = _supply_side(partial_gram) + RIDGE * identity_mat
     own_gram, own_rhs = (
         lax.psum_scatter(gram_acc, "rep", scatter_dimension=0, tiled=True),
         lax.psum_scatter(rhs_acc, "rep", scatter_dimension=0, tiled=True),

time: 526 us -> 441 us (0.84)
  waiting for transfers between devices: 270 us -> 189 us
  other arithmetic: 98.5 us -> 111 us
  matrix products: 39.3 us -> 27 us
  blocking collectives: 45.4 us -> 39.7 us
    psum x1 -> x0, waiting for transfers between devices: 187 us -> none  [shards(): added_term = lax.psum(partial_gram, ('ent', 'rep')) + RIDGE * identity_mat]
    all_gather x0 -> x1, waiting for transfers between devices: none -> 113 us  [shards(): _supply_side = lambda view: jnp.sum(lax.all_gather(view, ('ent', 'rep')), 0)]
    reduce_sum x0 -> x1, other arithmetic: none -> 13.1 us  [shards(): _supply_side = lambda view: jnp.sum(lax.all_gather(view, ('ent', 'rep')), 0)]
    unnamed x3, waiting for transfers between devices: 37.4 us -> 26.2 us
    dot_general x2, matrix products: 25 us -> 17.2 us  [accumulate(): gram_run = gram_run + jnp.dot(select_blk, run_gram, precision=highest)]
    all_to_all x1, blocking collectives: 30.5 us -> 24.9 us  [shards(): lax.all_to_all(run_factor.reshape(n_ent, slot_cap, seg_count * rank_width...]
  transfers between devices with their start and end apart: 4 -> 4, of which waited for: 3 -> 3; matrix products, arithmetic and copies ran while one was open for 17% -> 14% of each run, Pallas kernels for 0% -> 0%
where the time goes in v1:
time: 441 us
  waiting for transfers between devices  189 us (43%)
  other arithmetic  111 us (25%)
  blocking collectives  39.7 us (9%)
  local copies, waits for them, and re-layouts  30.5 us (7%)
  matrix products  27 us (6%)
  starting transfers between devices  26.4 us (6%)
  between operations  16.4 us (4%)
    all_gather x1, waiting for transfers between devices, shards(): _supply_side = lambda view: jnp.sum(lax.all_gather(view, ('ent', 'rep')), 0)  113 us
    all_to_all x1, waiting for transfers between devices, shards(): lax.all_to_all(picked.reshape(n_ent, slot_cap * tile_rows, rank_width), '...  50.2 us
    scatter-add x2, other arithmetic, spread(): jax.ops.segment_sum(contrib, item_blk.reshape(-1), num_segments=item_count)  45.1 us
    unnamed x3, waiting for transfers between devices  26.2 us
    all_to_all x1, blocking collectives, shards(): lax.all_to_all(run_factor.reshape(n_ent, slot_cap, seg_count * rank_width...  24.9 us
    gather x1, local copies, waits for them, and re-layouts, shards(): jnp.take(item_factors, item_ids.reshape(-1), axis=0)  24 us
    another operation x4, other arithmetic, solve_users(): lower = jnp.linalg.cholesky(gram)  23.6 us
    another operation x3, other arithmetic, solve_users(): lax.linalg.triangular_solve(lower, halfway, left_side=True, lower=True, t...  19.8 us
  transfers between devices with their start and end apart: 4, of which 3 were waited for; matrix products, arithmetic and copies ran while one was open for 14% of the time, Pallas kernels for 0%

profile of v1, /device:TPU:1, one launch (start us, length us, event | category | flops | bytes accessed | tf_op | source)
XLA Modules:
  0.0 440.6 jit_solution(17424386163869746797)
XLA Ops:
  10.0 24.0 %gather_fusion = bf16[8192,128]{1,0:T(8,128)(2,1)S(1)} fusion(bf16[1024,128]{1,0:T(8,128)(2,1)S(1)} %copy-done, s32[8192]{0:T(1024)S(1)} %broadcast_clamp_fusion), kind=kCustom, calls=%fused_computation | custom fusion | bytes 4227072 | tf_op jit(solution)/shard_map/jit(_take)/gather | solution.py:39
  34.1 4.6 %select_select_fusion = bf16[128,64,128]{2,1,0:T(8,128)(2,1)} fusion(bf16[128,64,128]{2,1,0:T(8,128)(2,1)S(1)} %bitcast.125, pred[128,64]{1,0:T(8,128)(4,1)S(1)} %compare_and_fusion, pred[128,64]{1,0:T(8,128)(4,1)S(1)} %copy.42), kind=kLoop, calls=%fused_computation.28 | loop fusion | flops 2097152 | bytes 4210688 | tf_op jit(solution)/shard_map/jit(_where)/select_n | solution.py:42
  38.6 18.6 %all-to-all-start = ((bf16[128,64,128]{2,1,0:T(8,128)(2,1)}), bf16[128,64,128]{2,1,0:T(8,128)(2,1)S(1)}, u32[]{:S(2)}, u32[]{:S(2)}) async-start(bf16[128,64,128]{2,1,0:T(8,128)(2,1)} %select_select_fusion), calls=%async_computation | async-start | bytes 4194304 | tf_op jit(solution)/shard_map/all_to_all | solution.py:43
  59.1 50.2 %all-to-all-done = bf16[128,64,128]{2,1,0:T(8,128)(2,1)S(1)} async-done(((bf16[128,64,128]{2,1,0:T(8,128)(2,1)}), bf16[128,64,128]{2,1,0:T(8,128)(2,1)S(1)}, u32[]{:S(2)}, u32[]{:S(2)}) %all-to-all-start) | async-done | bytes 2097184 | tf_op jit(solution)/shard_map/all_to_all | solution.py:43
  109.3 25.7 %while.24 = (s32[]{:T(128)}, f32[8,16384]{1,0:T(8,128)S(1)}, f32[8,128]{1,0:T(8,128)S(1)}, f32[2,8,128]{2,1,0:T(8,128)S(1)}, f32[2,128,32]{2,1,0:T(8,128)S(1)}, ...) while((s32[]{:T(128)}, f32[8,16384]{1,0:T(8,128)S(1)}, ...), condition=%wide.region_1.2_spmd.clone, body=%wide.region_0.1_spmd.clone.sunk | while | flops 345245696 | bytes 21267588 | solution.py:101
  110.5 2.9 fusion.49
  113.4 8.6 %convolution_add_fusion.4 = f32[8,16384]{1,0:T(8,128)S(1)} fusion(f32[16,8,128,128]{3,2,1,0:T(8,128)S(1)} %bitcast.122, f32[8,16384]{1,0:T(8,128)S(1)} %get-tuple-element.219, pred[]{:T(512)S(6)} %compare.15, f32[2,8,128]{2,1,0:T(8,128)S(1)} %get-tuple-element.230, s32[]{:T(128)S(6)} %copy.74), kind=kOutput, calls=%fused_computation.6.clone.1 | convolution fusion | flops 201588736 | bytes 9441285 | tf_op jit(solution)/shard_map/while/body/eval_jaxpr/dot_general | solution.py:87
  122.1 1.0 fusion.50
  123.2 2.9 fusion.49
  126.2 8.6 %convolution_add_fusion.4 = f32[8,16384]{1,0:T(8,128)S(1)} fusion(f32[16,8,128,128]{3,2,1,0:T(8,128)S(1)} %bitcast.122, f32[8,16384]{1,0:T(8,128)S(1)} %get-tuple-element.219, pred[]{:T(512)S(6)} %compare.15, f32[2,8,128]{2,1,0:T(8,128)S(1)} %get-tuple-element.230, s32[]{:T(128)S(6)} %copy.74), kind=kOutput, calls=%fused_computation.6.clone.1 | convolution fusion | flops 201588736 | bytes 9441285 | tf_op jit(solution)/shard_map/while/body/eval_jaxpr/dot_general | solution.py:87
  137.9 7.8 %all-to-all-start.1 = ((f32[128,2,32]{2,1,0:T(2,128)}), f32[128,2,32]{2,1,0:T(2,128)S(1)}, u32[]{:S(2)}, u32[]{:S(2)}) async-start(f32[128,2,32]{2,1,0:T(2,128)} %and_select_fusion), calls=%async_computation.1 | async-start | bytes 262144 | tf_op jit(solution)/shard_map/all_to_all | solution.py:125
  145.7 1.3 dynamic-slice
  147.7 9.1 %all-reduce.1 = f32[8,128]{1,0:T(8,128)S(1)} all-reduce(f32[8,128]{1,0:T(8,128)S(1)} %get-tuple-element.68), channel_id=4, replica_groups=mesh['ent'=128,'rep'=4] {'rep'}, use_global_device_ids=true, to_apply=%region_6.7.clone | all-reduce | flops 1024 | bytes 8192
  156.8 26.2 %all-reduce.4.cloned.1.call-done = f32[8,16384]{1,0:T(8,128)} async-done(((f32[8,16384]{1,0:T(8,128)}), f32[8,16384]{1,0:T(8,128)}) %all-reduce.4.cloned.1.call-update) | async-done | bytes 524304
  183.0 1.1 dynamic-slice_bitcast_fusion.2
  184.2 113.0 %all-gather.4.cloned.1.call-done = f32[65536,128]{1,0:T(8,128)} async-done(((f32[128,128]{1,0:T(8,128)}), f32[65536,128]{1,0:T(8,128)}) %all-gather.4.cloned.1.call-update) | async-done | bytes 33554448 | tf_op jit(solution)/shard_map/all_gather | solution.py:103
  297.2 13.1 %reduce_sum.9 = f32[128,128]{1,0:T(8,128)S(1)} reduce(f32[512,128,128]{2,1,0:T(8,128)} %bitcast.124, f32[]{:T(128)} %constant.109.clone.1), dimensions={0}, to_apply=%region_3.4 | reduce | flops 8372224 | bytes 33619972 | tf_op jit(solution)/shard_map/reduce_sum | solution.py:103
  310.6 23.5 %custom-call.9 = f32[2,128,128]{2,1,0:T(8,128)S(1)} custom-call(f32[2,128,128]{2,1,0:T(8,128)S(1)} %fusion.20), custom_call_target="Cholesky" | custom-call | tf_op jit(solution)/shard_map/jit(cholesky)/cholesky | solution.py:13
  334.3 19.7 %custom-call.10 = f32[2,1,128,128]{2,3,1,0:T(8,128)S(1)} custom-call(f32[2,1,128,128]{3,2,1,0:T(8,128)S(1)} %select_bitcast_fusion), custom_call_target="InvertDiagBlocksLowerTriangular" | custom-call | tf_op jit(solution)/shard_map/triangular_solve | solution.py:15
  354.5 5.7 %all-gather.1 = bf16[4,2,128]{2,1,0:T(2,128)(2,1)S(1)} all-gather(bf16[1,2,128]{2,1,0:T(2,128)(2,1)S(1)} %convert_bitcast_fusion), channel_id=1, replica_groups=mesh['ent'=128,'rep'=4] {'rep'}, dimensions={0}, use_global_device_ids=true | all-gather | bytes 2560 | tf_op jit(solution)/shard_map/all_gather | solution.py:110
  360.5 24.9 %all_to_all.15 = f32[128,2,128]{2,1,0:T(2,128)S(1)} all-to-all(f32[128,2,128]{2,1,0:T(2,128)S(1)} %bitcast.134), channel_id=1, replica_groups=mesh['ent'=128,'rep'=4] {'ent'}, dimensions={0} | all-to-all | bytes 262144 | tf_op jit(solution)/shard_map/all_to_all | solution.py:118
  385.4 46.8 %while.23 = (s32[]{:T(128)}, f32[1024,128]{1,0:T(8,128)S(1)}, s32[2,128,32]{2,1,0:T(8,128)S(1)}, f32[2,128,1,32]{3,1,2,0:T(8,128)S(1)}, f32[2,128,1,128]{3,1,2,0:T(8,128)S(1)}, /*index=5*/s32[]{:T(128)}) while((s32[]{:T(128)}, f32[1024,128]{1,0:T(8,128)S(1)}, s32[2,128,32]{2,1,0:T(8,128)S(1)}, f32[2,128,1,32]{3,1,2,0:T(8,128)S(1)}, ...), condition=%wide.region_9.10_spmd, body=%wide.region_7.9_spmd.sunk | while | flops 1048578 | bytes 8749145 | solution.py:147
  386.3 22.6 %scatter_fusion = f32[1024,128]{1,0:T(8,128)S(1)} fusion(f32[1024,128]{1,0:T(8,128)S(1)} %get-tuple-element.243, s32[4096]{0:T(1024)S(1)} %reshape.270, f32[4096,128]{1,0:T(8,128)S(1)} %bitcast_multiply_fusion.2), kind=kCustom, calls=%fused_computation.1.clone.1 | custom fusion | flops 524288 | bytes 6307840 | tf_op jit(solution)/shard_map/while/body/eval_jaxpr/scatter-add | solution.py:138
  409.7 22.6 %scatter_fusion = f32[1024,128]{1,0:T(8,128)S(1)} fusion(f32[1024,128]{1,0:T(8,128)S(1)} %get-tuple-element.243, s32[4096]{0:T(1024)S(1)} %reshape.270, f32[4096,128]{1,0:T(8,128)S(1)} %bitcast_multiply_fusion.2), kind=kCustom, calls=%fused_computation.1.clone.1 | custom fusion | flops 524288 | bytes 6307840 | tf_op jit(solution)/shard_map/while/body/eval_jaxpr/scatter-add | solution.py:138
  (84 shorter events, 12.0 us)
Async XLA Ops:
  8.0 2.0 copy-start
  38.6 19.1 %copy-start.5 = (s32[1,1,128]{2,1,0:T(1,128)S(1)}, s32[1,1,128]{2,1,0:T(1,128)}, u32[]{:S(2)}) copy-start(s32[1,1,128]{2,1,0:T(1,128)} %param.15) | copy-start | bytes 1540
  38.6 19.9 %copy-start.2 = (s32[1,1,256,32]{2,3,1,0:T(8,128)S(1)}, s32[1,1,256,32]{2,3,1,0:T(8,128)}, u32[]{:S(2)}) copy-start(s32[1,1,256,32]{2,3,1,0:T(8,128)} %param.14) | copy-start | bytes 98308
  38.6 20.4 %copy-start.3 = (s32[1,1,256,1]{2,3,1,0:T(1,128)S(1)}, s32[1,1,256,1]{2,3,1,0:T(1,128)}, u32[]{:S(2)}) copy-start(s32[1,1,256,1]{2,3,1,0:T(1,128)} %param.13) | copy-start | bytes 3076
  38.6 70.7 %all-to-all-start = ((bf16[128,64,128]{2,1,0:T(8,128)(2,1)}), bf16[128,64,128]{2,1,0:T(8,128)(2,1)S(1)}, u32[]{:S(2)}, u32[]{:S(2)}) async-start(bf16[128,64,128]{2,1,0:T(8,128)(2,1)} %select_select_fusion), calls=%async_computation | async-start | bytes 4194304 | tf_op jit(solution)/shard_map/all_to_all | solution.py:43
  57.2 125.8 %all-reduce.4.cloned.1.call-start = ((), (), s32[]{:S(2)}) async-start(), calls=%async_computation.4 | async-start | bytes 1048576
  135.0 0.8 copy-start.1
  135.8 161.4 %all-gather.4.cloned.1.call-start = ((), (), s32[]{:S(2)}) async-start(), calls=%async_computation.3 | async-start | bytes 33619968 | tf_op jit(solution)/shard_map/all_gather | solution.py:103
  137.9 222.6 %all-to-all-start.1 = ((f32[128,2,32]{2,1,0:T(2,128)}), f32[128,2,32]{2,1,0:T(2,128)S(1)}, u32[]{:S(2)}, u32[]{:S(2)}) async-start(f32[128,2,32]{2,1,0:T(2,128)} %and_select_fusion), calls=%async_computation.1 | async-start | bytes 262144 | tf_op jit(solution)/shard_map/all_to_all | solution.py:125
  354.5 30.9 %copy-start.4 = (f32[2,1,128]{2,1,0:T(1,128)}, f32[2,1,128]{2,1,0:T(1,128)S(1)}, u32[]{:S(2)}) copy-start(f32[2,1,128]{2,1,0:T(1,128)S(1)} %fusion.17) | copy-start | bytes 3076
Sparse Core Ops, SparseCore 0:
  135.9 46.9 all-reduce.3
Sparse Core Ops, SparseCore 1:
  140.7 156.4 all-gather.3
